TPU v7x, 32 devices: a whole 2x2x4 slice. The times are simulated.
32 devices in a mesh: grp: 2 (over y), ctx: 4 (over z), tp: 2 (over x), sub: 2 (over core).
Axes of the slice: x: 2, y: 2, z: 4, core: 2. Of those that a mesh axis runs over, the one named last changes fastest.
Arguments:
- context: bfloat16 [3072, 2048], P(('grp', 'ctx'), ('tp', 'sub')), parts along dimension 0, may hold values from -24 to 24
- context_pos: int32 [3072], P(('grp', 'ctx')), parts along dimension 0, may hold values from 0 to 1535, each once
- latent_in: bfloat16 [64, 2048], P(('grp', 'ctx')), parts along dimension 0, may hold values from -24 to 24
- latent_start: int32 [2], P('grp'), parts along dimension 0, may hold values from 768 to 1504
- ctx_gain: float32 [2048], replicated, may hold values from 0.25 to 1.75
- lat_gain: float32 [2048], replicated, may hold values from 0.25 to 1.75
- mid_gain: float32 [2048], replicated, may hold values from 0.25 to 1.75
- cross_q: bfloat16 [2048, 2048], P('ctx', ('tp', 'sub')), may hold values from -2 to 2
- cross_k: bfloat16 [2048, 2048], P('ctx', ('tp', 'sub')), may hold values from -2 to 2
- cross_v: bfloat16 [2048, 2048], P('ctx', ('tp', 'sub')), may hold values from -0.125 to 0.125
- cross_out: bfloat16 [2048, 2048], P('ctx', ('tp', 'sub')), may hold values from -0.125 to 0.125
- self_qkv: bfloat16 [2048, 3, 2048], P('ctx', None, ('tp', 'sub')), may hold values from -2 to 2
- self_out: bfloat16 [2048, 2048], P('ctx', ('tp', 'sub')), may hold values from -0.125 to 0.125
Outputs:
- latent_out: bfloat16 [64, 2048], P(('grp', 'ctx'), ('tp', 'sub')), parts along dimension 0
There are 2 independent parts, one for each index of `grp`. A program takes and returns all parts, laid end to end along the dimension named above; an argument that names none is the same for every part. Nothing has to cross between parts.
Inputs may be any that keep to these rules, and one draw needn't show every extreme that they name: context_pos holds each of 0 to 1535 once.
All inputs are finite; a program needn't handle non-finite values.
Results may differ from a plain program's by a relative error of at most 0.035.
Values may be sent and summed in bfloat16 or wider, within the bound.
A program may use at most 64 MiB of HBM per device.

v0:
```python
import math
import jax
import jax.numpy as jnp
from jax import lax
from jax.sharding import PartitionSpec as P

DH = 128
EPS = 1e-05
NEG = -1e30


def combined_all(shard, axis, combine):
    everything = jax.tree.map(
        lambda part, kind: lax.all_gather(part.astype(kind), axis),
        shard,
        (jnp.bfloat16, jnp.bfloat16, jnp.bfloat16),
    )

    def take(k):
        return jax.tree.map(lambda part, own: part[k].astype(own.dtype), everything, shard)

    return lax.fori_loop(
        1, lax.axis_size(axis), lambda k, so_far: combine(so_far, take(k)), take(0)
    )


def rms_rows(values, gain):
    wide = values.astype(jnp.float32)
    scale = lax.rsqrt(jnp.mean(wide * wide, axis=-1, keepdims=True) + EPS)
    return (wide * scale * gain).astype(jnp.bfloat16)


def contract_last(left, right):
    return lax.dot_general(
        left, right, (((1,), (1,)), ((), ())), preferred_element_type=jnp.float32
    )


def softmax_parts(queries, keys, values, allowed):
    heads = queries.shape[1] // DH
    maxima = []
    totals = []
    numerators = []
    for head in range(heads):
        begin = head * DH
        scores = contract_last(queries[:, begin : begin + DH], keys[:, begin : begin + DH]) * (
            1.0 / math.sqrt(DH)
        )
        scores = jnp.where(allowed, scores, NEG)
        top = jnp.max(scores, axis=1)
        weights = jnp.where(allowed, jnp.exp(scores - top[:, None]), 0.0)
        maxima.append(top)
        totals.append(jnp.sum(weights, axis=1))
        numerators.append(
            jnp.dot(
                weights.astype(jnp.bfloat16),
                values[:, begin : begin + DH],
                preferred_element_type=jnp.float32,
            )
        )
    return (
        jnp.stack(maxima, axis=1),
        jnp.stack(totals, axis=1),
        jnp.concatenate(numerators, axis=1),
    )


def combine_parts(first, second):
    top = jnp.maximum(first[0], second[0])
    first_factor = jnp.exp(first[0] - top)
    second_factor = jnp.exp(second[0] - top)
    totals = first[1] * first_factor + second[1] * second_factor
    numerators = first[2] * jnp.repeat(first_factor, DH, axis=1) + second[2] * jnp.repeat(
        second_factor, DH, axis=1
    )
    return (top, totals, numerators)


def on_device(
    context,
    context_pos,
    latent_in,
    latent_start,
    ctx_gain,
    lat_gain,
    mid_gain,
    cross_q,
    cross_k,
    cross_v,
    cross_out,
    self_qkv,
    self_out,
):
    owned = latent_in.shape[0]
    columns = cross_q.shape[1]
    whole = lax.all_gather(context, ("tp", "sub"), axis=1, tiled=True)
    normed_ctx = rms_rows(whole, ctx_gain)
    normed_lat = rms_rows(latent_in, lat_gain)
    query_sum = jnp.dot(
        normed_lat,
        lax.all_gather(cross_q, "ctx", axis=0, tiled=True),
        preferred_element_type=jnp.float32,
    )
    key_sum = jnp.dot(
        normed_ctx,
        lax.all_gather(cross_k, "ctx", axis=0, tiled=True),
        preferred_element_type=jnp.float32,
    )
    value_sum = jnp.dot(
        normed_ctx,
        lax.all_gather(cross_v, "ctx", axis=0, tiled=True),
        preferred_element_type=jnp.float32,
    )
    keys = key_sum.astype(jnp.bfloat16)
    values = value_sum.astype(jnp.bfloat16)
    queries = lax.all_gather(query_sum.astype(jnp.bfloat16), "ctx", axis=0, tiled=True)
    query_pos = latent_start[0] + jnp.arange(queries.shape[0], dtype=jnp.int32)
    allowed = context_pos[None, :] <= query_pos[:, None]
    maxima, totals, numerators = softmax_parts(queries, keys, values, allowed)
    first_row = lax.axis_index("ctx") * owned
    maxima, totals, numerators = combined_all((maxima, totals, numerators), "ctx", combine_parts)
    totals = lax.dynamic_slice_in_dim(totals, first_row, owned, 0)
    numerators = lax.dynamic_slice_in_dim(numerators, first_row, owned, 0)
    attended = (numerators / jnp.repeat(totals, DH, axis=1)).astype(jnp.bfloat16)
    cross_terms = contract_last(attended, lax.all_gather(cross_out, "ctx", axis=0, tiled=True))
    cross_sum = lax.psum(cross_terms.astype(jnp.bfloat16), ("tp", "sub")).astype(jnp.float32)
    hidden = (latent_in.astype(jnp.float32) + cross_sum).astype(jnp.bfloat16)
    normed_mid = rms_rows(hidden, mid_gain)
    piece = lax.all_gather(self_qkv, "ctx", axis=0, tiled=True)
    span = piece.shape[0]
    projected = jnp.dot(
        normed_mid, piece.reshape(span, 3 * columns), preferred_element_type=jnp.float32
    )
    projected = projected.astype(jnp.bfloat16).reshape(owned, 3, columns)
    gathered = lax.all_gather(projected[:, 1:], "ctx", axis=0, tiled=True)
    key_index = jnp.arange(gathered.shape[0], dtype=jnp.int32)
    row_index = first_row + jnp.arange(owned, dtype=jnp.int32)
    causal = key_index[None, :] <= row_index[:, None]
    unused, self_totals, self_numerators = softmax_parts(
        projected[:, 0], gathered[:, 0], gathered[:, 1], causal
    )
    attended_self = (self_numerators / jnp.repeat(self_totals, DH, axis=1)).astype(jnp.bfloat16)
    self_terms = contract_last(attended_self, lax.all_gather(self_out, "ctx", axis=0, tiled=True))
    summed = lax.psum_scatter(
        self_terms.astype(jnp.bfloat16), ("tp", "sub"), scatter_dimension=1, tiled=True
    ).astype(jnp.float32)
    share = summed.shape[1]
    residual = lax.dynamic_slice_in_dim(hidden, lax.axis_index(("tp", "sub")) * share, share, 1)
    return (residual.astype(jnp.float32) + summed).astype(jnp.bfloat16)


def solution(mesh):
    return jax.shard_map(
        on_device,
        mesh=mesh,
        in_specs=(
            P(("grp", "ctx"), ("tp", "sub")),
            P(("grp", "ctx")),
            P(("grp", "ctx"), None),
            P("grp"),
            P(),
            P(),
            P(),
            P("ctx", ("tp", "sub")),
            P("ctx", ("tp", "sub")),
            P("ctx", ("tp", "sub")),
            P("ctx", ("tp", "sub")),
            P("ctx", None, ("tp", "sub")),
            P("ctx", ("tp", "sub")),
        ),
        out_specs=P(("grp", "ctx"), ("tp", "sub")),
        check_vma=False,
    )
```

profile of v0, /device:TPU:0, one launch (start us, length us, event | category | flops | bytes accessed | tf_op | source)
XLA Modules:
  0.0 410.3 jit_solution(3761533873180696968)
XLA Ops:
  6.5 0.7 all-gather.10.cloned.1.call-update
  7.3 0.7 all-gather.8.cloned.1.call-update
  8.1 0.7 all-gather.12.cloned.1.call-update
  8.8 0.5 all-gather.14.cloned.1.call-update
  9.4 0.5 all-gather.16.cloned.1.call-update
  10.0 1.6 copy.21
  11.7 0.7 all-gather.20.cloned.1.call-update
  13.2 18.1 %all-gather.10.cloned.1.call-done = bf16[384,2048]{1,0:T(8,128)(2,1)} async-done(((bf16[384,512]{1,0:T(8,128)(2,1)}), bf16[384,2048]{1,0:T(8,128)(2,1)}) %all-gather.10.cloned.1.call-update) | async-done | bytes 1572880 | tf_op jit(solution)/shard_map/all_gather | solution.py:96
  31.3 1.9 fusion.3
  33.2 45.6 %all-gather.8.cloned.1.call-done = bf16[2048,512]{1,0:T(8,128)(2,1)} async-done(((bf16[512,512]{1,0:T(8,128)(2,1)}), bf16[2048,512]{1,0:T(8,128)(2,1)}) %all-gather.8.cloned.1.call-update) | async-done | bytes 2097168 | tf_op jit(solution)/shard_map/all_gather | solution.py:101
  78.9 2.0 convolution_convert_fusion.9
  80.9 13.3 %all_gather.40 = bf16[32,512]{1,0:T(8,128)(2,1)S(1)} all-gather(bf16[8,512]{1,0:T(8,128)(2,1)S(1)} %convolution_convert_fusion.9), channel_id=1, replica_groups=mesh['grp'=2,'ctx'=4,'tp'=2,'sub'=2] {'ctx'}, dimensions={0}, use_global_device_ids=true | all-gather | bytes 40960 | tf_op jit(solution)/shard_map/all_gather | solution.py:116
  94.2 31.1 %all-gather.12.cloned.1.call-done = bf16[2048,512]{1,0:T(8,128)(2,1)} async-done(((bf16[512,512]{1,0:T(8,128)(2,1)}), bf16[2048,512]{1,0:T(8,128)(2,1)}) %all-gather.12.cloned.1.call-update) | async-done | bytes 2097168 | tf_op jit(solution)/shard_map/all_gather | solution.py:106
  125.3 2.6 convolution_convert_fusion.4
  127.9 0.3 fusion.137
  128.4 0.3 fusion.135
  129.0 42.7 %all-gather.14.cloned.1.call-done = bf16[2048,512]{1,0:T(8,128)(2,1)} async-done(((bf16[512,512]{1,0:T(8,128)(2,1)}), bf16[2048,512]{1,0:T(8,128)(2,1)}) %all-gather.14.cloned.1.call-update) | async-done | bytes 2097168 | tf_op jit(solution)/shard_map/all_gather | solution.py:111
  171.7 2.6 convolution_convert_fusion.3
  175.4 14.4 %all_gather.46 = bf16[4,32,512]{2,1,0:T(8,128)(2,1)S(1)} all-gather(bf16[1,32,512]{2,1,0:T(8,128)(2,1)S(1)} %pad_maximum_fusion), channel_id=1, replica_groups=mesh['grp'=2,'ctx'=4,'tp'=2,'sub'=2] {'ctx'}, dimensions={0}, use_global_device_ids=true | all-gather | bytes 163840 | tf_op jit(solution)/shard_map/all_gather | solution.py:14
  189.9 8.6 %all_gather.44 = bf16[4,32,4]{1,2,0:T(4,128)(2,1)S(1)} all-gather(bf16[1,32,4]{1,2,0:T(4,128)(2,1)S(1)} %pad_maximum_fusion.3), channel_id=1, replica_groups=mesh['grp'=2,'ctx'=4,'tp'=2,'sub'=2] {'ctx'}, dimensions={0}, use_global_device_ids=true | all-gather | bytes 1280 | tf_op jit(solution)/shard_map/all_gather | solution.py:14
  198.5 9.3 %all_gather.43 = bf16[4,32,4]{1,2,0:T(4,128)(2,1)S(1)} all-gather(bf16[1,32,4]{1,2,0:T(4,128)(2,1)S(1)} %pad_maximum_fusion.2), channel_id=1, replica_groups=mesh['grp'=2,'ctx'=4,'tp'=2,'sub'=2] {'ctx'}, dimensions={0}, use_global_device_ids=true | all-gather | bytes 1280 | tf_op jit(solution)/shard_map/all_gather | solution.py:14
  207.8 1.3 while.19
  209.2 9.8 %all-gather.16.cloned.1.call-done = bf16[2048,512]{1,0:T(8,128)(2,1)} async-done(((bf16[512,512]{1,0:T(8,128)(2,1)}), bf16[2048,512]{1,0:T(8,128)(2,1)}) %all-gather.16.cloned.1.call-update) | async-done | bytes 2097168 | tf_op jit(solution)/shard_map/all_gather | solution.py:125
  219.0 2.2 convolution_convert_fusion.2
  221.3 11.4 %psum.7 = bf16[8,2048]{1,0:T(8,128)(2,1)S(1)} all-reduce(bf16[8,2048]{1,0:T(8,128)(2,1)S(1)} %convolution_convert_fusion.2), channel_id=1, replica_groups=mesh['grp'=2,'ctx'=4,'tp'=2,'sub'=2] {'tp','sub'}, use_global_device_ids=true, to_apply=%region_12.13 | all-reduce | flops 16384 | bytes 65536 | tf_op jit(solution)/shard_map/psum | solution.py:126
  232.8 101.9 %all-gather.18.cloned.1.call-done = bf16[2048,3,512]{0,2,1:T(8,128)(2,1)} async-done(((bf16[512,3,512]{0,2,1:T(8,128)(2,1)}), bf16[2048,3,512]{0,2,1:T(8,128)(2,1)}) %all-gather.18.cloned.1.call-update) | async-done | bytes 6291472 | tf_op jit(solution)/shard_map/all_gather | solution.py:129
  334.8 4.5 %convolution_convert_fusion.1 = bf16[8,1536]{1,0:T(8,128)(2,1)S(1)} fusion(bf16[2048,1536]{0,1:T(8,128)(2,1)} %bitcast.107, bf16[8,2048]{1,0:T(8,128)(2,1)S(1)} %get-tuple-element.211, f32[2048]{0:T(1024)S(1)} %copy-done.4, f32[8]{0:T(128)S(1)} %add_rsqrt_fusion.1), kind=kOutput, calls=%fused_computation.16 | convolution fusion | flops 50409472 | bytes 6357024 | tf_op jit(solution)/shard_map/dot_general | solution.py:131
  339.3 13.6 %all_gather.49 = bf16[32,2,512]{2,0,1:T(8,128)(2,1)S(1)} all-gather(bf16[8,2,512]{2,0,1:T(8,128)(2,1)S(1)} %slice.141), channel_id=1, replica_groups=mesh['grp'=2,'ctx'=4,'tp'=2,'sub'=2] {'ctx'}, dimensions={0}, use_global_device_ids=true | all-gather | bytes 81920 | tf_op jit(solution)/shard_map/all_gather | solution.py:135
  354.8 26.4 %all-gather.20.cloned.1.call-done = bf16[2048,512]{1,0:T(8,128)(2,1)} async-done(((bf16[512,512]{1,0:T(8,128)(2,1)}), bf16[2048,512]{1,0:T(8,128)(2,1)}) %all-gather.20.cloned.1.call-update) | async-done | bytes 2097168 | tf_op jit(solution)/shard_map/all_gather | solution.py:143
  381.2 2.9 convolution_convert_fusion
  384.1 18.1 %reduce-scatter.2.cloned.1.call-done = bf16[8,512]{1,0:T(8,128)(2,1)} async-done(((bf16[8,2048]{1,0:T(8,128)(2,1)}), bf16[8,512]{1,0:T(8,128)(2,1)}) %reduce-scatter.2.cloned.1.call-update) | async-done | bytes 8208 | tf_op jit(solution)/shard_map/reduce_scatter | solution.py:144
  402.2 1.3 add_convert_fusion
  (78 shorter events, 5.5 us)
Async XLA Ops:
  6.5 3.4 copy-start
  6.5 24.8 %all-gather.10.cloned.1.call-start = ((), (), s32[]{:S(2)}) async-start(), calls=%async_computation.2 | async-start | bytes 1966080 | tf_op jit(solution)/shard_map/all_gather | solution.py:96
  7.3 71.6 %all-gather.8.cloned.1.call-start = ((), (), s32[]{:S(2)}) async-start(), calls=%async_computation.1 | async-start | bytes 2621440 | tf_op jit(solution)/shard_map/all_gather | solution.py:101
  8.0 117.3 %all-gather.12.cloned.1.call-start = ((), (), s32[]{:S(2)}) async-start(), calls=%async_computation.3 | async-start | bytes 2621440 | tf_op jit(solution)/shard_map/all_gather | solution.py:106
  8.7 162.9 %all-gather.14.cloned.1.call-start = ((), (), s32[]{:S(2)}) async-start(), calls=%async_computation.4 | async-start | bytes 2621440 | tf_op jit(solution)/shard_map/all_gather | solution.py:111
  9.3 209.7 %all-gather.16.cloned.1.call-start = ((), (), s32[]{:S(2)}) async-start(), calls=%async_computation.5 | async-start | bytes 2621440 | tf_op jit(solution)/shard_map/all_gather | solution.py:125
  9.9 3.2 copy-start.2
  9.9 324.8 %all-gather.18.cloned.1.call-start = ((), (), s32[]{:S(2)}) async-start(), calls=%async_computation.6 | async-start | bytes 7864320 | tf_op jit(solution)/shard_map/all_gather | solution.py:129
  11.6 67.3 %copy-start.3 = (f32[2048]{0:T(1024)S(1)}, f32[2048]{0:T(1024)}, u32[]{:S(2)}) copy-start(f32[2048]{0:T(1024)} %param.20) | copy-start | bytes 24580
  11.6 113.7 %copy-start.6 = (f32[2048]{0:T(1024)S(1)}, f32[2048]{0:T(1024)}, u32[]{:S(2)}) copy-start(f32[2048]{0:T(1024)} %param.19) | copy-start | bytes 24580
  11.6 369.6 %all-gather.20.cloned.1.call-start = ((), (), s32[]{:S(2)}) async-start(), calls=%async_computation.7 | async-start | bytes 2621440 | tf_op jit(solution)/shard_map/all_gather | solution.py:143
  12.4 389.8 %reduce-scatter.2.cloned.1.call-start = ((), (), s32[]{:S(2)}) async-start(), calls=%async_computation.8 | async-start | bytes 40960 | tf_op jit(solution)/shard_map/reduce_scatter | solution.py:144
  31.3 94.0 %copy-start.1 = (bf16[384,2048]{1,0:T(8,128)(2,1)S(1)}, bf16[384,2048]{1,0:T(8,128)(2,1)}, u32[]{:S(2)}) copy-start(bf16[384,2048]{1,0:T(8,128)(2,1)} %all-gather.10.cloned.1.call-done) | copy-start | bytes 4718596
  94.2 33.7 %copy-start.5 = (s32[384]{0:T(512)S(1)}, s32[384]{0:T(512)}, u32[]{:S(2)}) copy-start(s32[384]{0:T(512)} %param.16) | copy-start | bytes 4612
  207.8 127.0 %copy-start.4 = (f32[2048]{0:T(1024)S(1)}, f32[2048]{0:T(1024)}, u32[]{:S(2)}) copy-start(f32[2048]{0:T(1024)} %param.21) | copy-start | bytes 24580
Sparse Core Ops, SparseCore 0:
  8.9 22.3 all-gather.9
  32.9 45.9 all-gather.7
  80.4 44.7 all-gather.11
  126.7 44.9 all-gather.13
  173.1 45.9 all-gather.15
  220.5 114.2 all-gather.17
  336.3 44.8 all-gather.19
  384.2 17.9 reduce-scatter.1
where the time goes:
time: 411 us; the launch traced here: 410 us
  waiting for transfers between devices  298 us (73%)
  blocking collectives  70.6 us (17%)
  matrix products  20.4 us (5%)
  between operations  14.3 us (3%)
  other arithmetic  4.19 us (1%)
    all_gather x1, waiting for transfers between devices, on_device(): piece = lax.all_gather(self_qkv, 'ctx', axis=0, tiled=True)  102 us
    all_gather x1, waiting for transfers between devices, on_device(): lax.all_gather(cross_q, 'ctx', axis=0, tiled=True)  45.6 us
    all_gather x1, waiting for transfers between devices, on_device(): lax.all_gather(cross_v, 'ctx', axis=0, tiled=True)  42.7 us
    all_gather x3, blocking collectives, combined_all(): lax.all_gather(part.astype(kind), axis)  32.3 us
    all_gather x1, waiting for transfers between devices, on_device(): lax.all_gather(cross_k, 'ctx', axis=0, tiled=True)  31.1 us
    all_gather x1, waiting for transfers between devices, on_device(): lax.all_gather(self_out, 'ctx', axis=0, tiled=True)  26.4 us
    reduce_scatter x1, waiting for transfers between devices, on_device(): lax.psum_scatter(self_terms.astype(jnp.bfloat16), ('tp', 'sub'), scatter_...  18.1 us
    all_gather x1, waiting for transfers between devices, on_device(): whole = lax.all_gather(context, ('tp', 'sub'), axis=1, tiled=True)  18.1 us
  transfers between devices with their start and end apart: 8, of which 8 were waited for; matrix products, arithmetic and copies ran while one was open for 6% of the time, Pallas kernels for 0%

commit v1 on v0

--- a/solution.py
+++ b/solution.py
@@ -7,6 +7,28 @@
 DH = 128
 EPS = 1e-05
 NEG = -1e30
+
+
+def joined_along(tiles, dim):
+    shape = list(tiles.shape[1:])
+    shape[dim] *= tiles.shape[0]
+    return jnp.moveaxis(tiles, 0, dim).reshape(shape)
+
+
+def collect(x, axis, dim):
+    count = lax.axis_size(axis)
+    pairs = [(i, (i + 1) % count) for i in range(count)]
+    back = [(b, a) for a, b in pairs]
+    lower, upper = ([], [])
+    for step in range(count - 1):
+        if step % 2 == 0:
+            lower.append(lax.ppermute(lower[-1] if lower else x, axis, pairs))
+        else:
+            upper.append(lax.ppermute(upper[-1] if upper else x, axis, back))
+    pieces = jnp.stack([*lower[::-1], x, *upper])
+    shift = lax.axis_index(axis) - len(lower)
+    pieces = pieces[(jnp.arange(count) - shift) % count]
+    return joined_along(pieces, dim)
 
 
 def combined_all(shard, axis, combine):
@@ -96,11 +118,7 @@
     whole = lax.all_gather(context, ("tp", "sub"), axis=1, tiled=True)
     normed_ctx = rms_rows(whole, ctx_gain)
     normed_lat = rms_rows(latent_in, lat_gain)
-    query_sum = jnp.dot(
-        normed_lat,
-        lax.all_gather(cross_q, "ctx", axis=0, tiled=True),
-        preferred_element_type=jnp.float32,
-    )
+    query_sum = jnp.dot(normed_lat, collect(cross_q, "ctx", 0), preferred_element_type=jnp.float32)
     key_sum = jnp.dot(
         normed_ctx,
         lax.all_gather(cross_k, "ctx", axis=0, tiled=True),

time: 411 us -> 371 us (0.903)
  waiting for transfers between devices: 298 us -> 239 us
  blocking collectives: 70.6 us -> 80.1 us
  starting transfers between devices: 0.27 us -> 5.41 us
    all_gather x1 -> x0, waiting for transfers between devices: 45.6 us -> none  [on_device(): lax.all_gather(cross_q, 'ctx', axis=0, tiled=True)]
    ppermute x0 -> x3, waiting for transfers between devices: none -> 41.2 us  [the longest x2 31.4 us: collect(): lower.append(lax.ppermute(lower[-1] if lower else x, axis, pairs))]
    all_gather x1, waiting for transfers between devices: 31.1 us -> 0.02 us  [on_device(): lax.all_gather(cross_k, 'ctx', axis=0, tiled=True)]
    all_gather x1, waiting for transfers between devices: 18.1 us -> 0.01 us  [on_device(): whole = lax.all_gather(context, ('tp', 'sub'), axis=1, tiled=True)]
    all_gather x1, blocking collectives: 13.3 us -> 22.8 us  [on_device(): lax.all_gather(query_sum.astype(jnp.bfloat16), 'ctx', axis=0, tiled=True)]
    ppermute x0 -> x3, starting transfers between devices: none -> 5.17 us  [the longest x2 3.08 us: collect(): lower.append(lax.ppermute(lower[-1] if lower else x, axis, pairs))]
  transfers between devices with their start and end apart: 8 -> 10, of which waited for: 8 -> 8; matrix products, arithmetic and copies ran while one was open for 6% -> 7% of each run, Pallas kernels for 0% -> 0%
where the time goes in v1:
time: 371 us
  waiting for transfers between devices  239 us (64%)
  blocking collectives  80.1 us (22%)
  matrix products  21 us (6%)
  between operations  14.4 us (4%)
  starting transfers between devices  5.41 us (1%)
  other arithmetic  5.4 us (1%)
  local copies, waits for them, and re-layouts  4.8 us (1%)
    all_gather x1, waiting for transfers between devices, on_device(): piece = lax.all_gather(self_qkv, 'ctx', axis=0, tiled=True)  102 us
    all_gather x1, waiting for transfers between devices, on_device(): lax.all_gather(cross_v, 'ctx', axis=0, tiled=True)  39.4 us
    all_gather x3, blocking collectives, combined_all(): lax.all_gather(part.astype(kind), axis)  32.3 us
    ppermute x2, waiting for transfers between devices, collect(): lower.append(lax.ppermute(lower[-1] if lower else x, axis, pairs))  31.4 us
    all_gather x1, waiting for transfers between devices, on_device(): lax.all_gather(self_out, 'ctx', axis=0, tiled=True)  26.1 us
    all_gather x1, blocking collectives, on_device(): lax.all_gather(query_sum.astype(jnp.bfloat16), 'ctx', axis=0, tiled=True)  22.8 us
    reduce_scatter x1, waiting for transfers between devices, on_device(): lax.psum_scatter(self_terms.astype(jnp.bfloat16), ('tp', 'sub'), scatter_...  18.3 us
    all_gather x1, blocking collectives, on_device(): gathered = lax.all_gather(projected[:, 1:], 'ctx', axis=0, tiled=True)  13.6 us
  transfers between devices with their start and end apart: 10, of which 8 were waited for; matrix products, arithmetic and copies ran while one was open for 7% of the time, Pallas kernels for 0%

profile of v1, /device:TPU:0, one launch (start us, length us, event | category | flops | bytes accessed | tf_op | source)
XLA Modules:
  0.0 370.6 jit_solution(16252477635154419502)
XLA Ops:
  6.5 0.7 all-gather.7.cloned.1.call-update
  7.3 0.7 all-gather.9.cloned.1.call-update
  8.1 0.7 all-gather.11.cloned.1.call-update
  8.8 0.5 all-gather.13.cloned.1.call-update
  9.4 1.6 copy.21
  11.1 3.1 collective-permute-start
  14.1 2.1 collective-permute-start.2
  17.0 12.0 %collective-permute-done = bf16[512,512]{1,0:T(8,128)(2,1)S(1)} collective-permute-done((bf16[512,512]{1,0:T(8,128)(2,1)S(1)}, bf16[512,512]{1,0:T(8,128)(2,1)S(1)}, u32[]{:S(2)}, u32[]{:S(2)}) %collective-permute-start) | collective-permute-done | bytes 524320 | tf_op jit(solution)/shard_map/ppermute | solution.py:25
  29.1 9.9 %collective-permute-done.2 = bf16[512,512]{1,0:T(8,128)(2,1)S(1)} collective-permute-done((bf16[512,512]{1,0:T(8,128)(2,1)S(1)}, bf16[512,512]{1,0:T(8,128)(2,1)S(1)}, u32[]{:S(2)}, u32[]{:S(2)}) %collective-permute-start.2) | collective-permute-done | bytes 524320 | tf_op jit(solution)/shard_map/ppermute | solution.py:27
  39.0 19.4 %collective-permute-done.1 = bf16[512,512]{1,0:T(8,128)(2,1)S(1)} collective-permute-done((bf16[512,512]{1,0:T(8,128)(2,1)S(1)}, bf16[512,512]{1,0:T(8,128)(2,1)S(1)}, u32[]{:S(2)}, u32[]{:S(2)}) %collective-permute-start.1) | collective-permute-done | bytes 524320 | tf_op jit(solution)/shard_map/ppermute | solution.py:25
  58.4 1.3 pad_maximum_fusion
  59.7 2.0 gather_fusion
  61.7 2.0 convolution_convert_fusion.9
  63.8 22.8 %all_gather.36 = bf16[32,512]{1,0:T(8,128)(2,1)S(1)} all-gather(bf16[8,512]{1,0:T(8,128)(2,1)S(1)} %convolution_convert_fusion.9), channel_id=1, replica_groups=mesh['grp'=2,'ctx'=4,'tp'=2,'sub'=2] {'ctx'}, dimensions={0}, use_global_device_ids=true | all-gather | bytes 40960 | tf_op jit(solution)/shard_map/all_gather | solution.py:134
  86.6 1.8 fusion.3
  88.4 3.2 convolution_convert_fusion.4
  92.7 39.4 %all-gather.11.cloned.1.call-done = bf16[2048,512]{1,0:T(8,128)(2,1)} async-done(((bf16[512,512]{1,0:T(8,128)(2,1)}), bf16[2048,512]{1,0:T(8,128)(2,1)}) %all-gather.11.cloned.1.call-update) | async-done | bytes 2097168 | tf_op jit(solution)/shard_map/all_gather | solution.py:129
  132.1 2.6 convolution_convert_fusion.3
  135.8 14.4 %all_gather.42 = bf16[4,32,512]{2,1,0:T(8,128)(2,1)S(1)} all-gather(bf16[1,32,512]{2,1,0:T(8,128)(2,1)S(1)} %pad_maximum_fusion.1), channel_id=1, replica_groups=mesh['grp'=2,'ctx'=4,'tp'=2,'sub'=2] {'ctx'}, dimensions={0}, use_global_device_ids=true | all-gather | bytes 163840 | tf_op jit(solution)/shard_map/all_gather | solution.py:36
  150.3 8.6 %all_gather.40 = bf16[4,32,4]{1,2,0:T(4,128)(2,1)S(1)} all-gather(bf16[1,32,4]{1,2,0:T(4,128)(2,1)S(1)} %pad_maximum_fusion.4), channel_id=1, replica_groups=mesh['grp'=2,'ctx'=4,'tp'=2,'sub'=2] {'ctx'}, dimensions={0}, use_global_device_ids=true | all-gather | bytes 1280 | tf_op jit(solution)/shard_map/all_gather | solution.py:36
  158.9 9.3 %all_gather.39 = bf16[4,32,4]{1,2,0:T(4,128)(2,1)S(1)} all-gather(bf16[1,32,4]{1,2,0:T(4,128)(2,1)S(1)} %pad_maximum_fusion.3), channel_id=1, replica_groups=mesh['grp'=2,'ctx'=4,'tp'=2,'sub'=2] {'ctx'}, dimensions={0}, use_global_device_ids=true | all-gather | bytes 1280 | tf_op jit(solution)/shard_map/all_gather | solution.py:36
  168.2 1.3 while.19
  169.6 9.8 %all-gather.13.cloned.1.call-done = bf16[2048,512]{1,0:T(8,128)(2,1)} async-done(((bf16[512,512]{1,0:T(8,128)(2,1)}), bf16[2048,512]{1,0:T(8,128)(2,1)}) %all-gather.13.cloned.1.call-update) | async-done | bytes 2097168 | tf_op jit(solution)/shard_map/all_gather | solution.py:143
  179.5 2.2 convolution_convert_fusion.2
  181.7 11.4 %psum.7 = bf16[8,2048]{1,0:T(8,128)(2,1)S(1)} all-reduce(bf16[8,2048]{1,0:T(8,128)(2,1)S(1)} %convolution_convert_fusion.2), channel_id=1, replica_groups=mesh['grp'=2,'ctx'=4,'tp'=2,'sub'=2] {'tp','sub'}, use_global_device_ids=true, to_apply=%region_12.13 | all-reduce | flops 16384 | bytes 65536 | tf_op jit(solution)/shard_map/psum | solution.py:144
  193.2 101.9 %all-gather.15.cloned.1.call-done = bf16[2048,3,512]{0,2,1:T(8,128)(2,1)} async-done(((bf16[512,3,512]{0,2,1:T(8,128)(2,1)}), bf16[2048,3,512]{0,2,1:T(8,128)(2,1)}) %all-gather.15.cloned.1.call-update) | async-done | bytes 6291472 | tf_op jit(solution)/shard_map/all_gather | solution.py:147
  295.2 4.5 %convolution_convert_fusion.1 = bf16[8,1536]{1,0:T(8,128)(2,1)S(1)} fusion(bf16[2048,1536]{0,1:T(8,128)(2,1)} %bitcast.115, bf16[8,2048]{1,0:T(8,128)(2,1)S(1)} %get-tuple-element.211, f32[2048]{0:T(1024)S(1)} %copy-done.6, f32[8]{0:T(128)S(1)} %add_rsqrt_fusion.1), kind=kOutput, calls=%fused_computation.17 | convolution fusion | flops 50409472 | bytes 6357024 | tf_op jit(solution)/shard_map/dot_general | solution.py:149
  299.7 13.6 %all_gather.45 = bf16[32,2,512]{2,0,1:T(8,128)(2,1)S(1)} all-gather(bf16[8,2,512]{2,0,1:T(8,128)(2,1)S(1)} %slice.143), channel_id=1, replica_groups=mesh['grp'=2,'ctx'=4,'tp'=2,'sub'=2] {'ctx'}, dimensions={0}, use_global_device_ids=true | all-gather | bytes 81920 | tf_op jit(solution)/shard_map/all_gather | solution.py:153
  315.2 26.1 %all-gather.17.cloned.1.call-done = bf16[2048,512]{1,0:T(8,128)(2,1)} async-done(((bf16[512,512]{1,0:T(8,128)(2,1)}), bf16[2048,512]{1,0:T(8,128)(2,1)}) %all-gather.17.cloned.1.call-update) | async-done | bytes 2097168 | tf_op jit(solution)/shard_map/all_gather | solution.py:161
  341.3 2.9 convolution_convert_fusion
  344.2 18.3 %reduce-scatter.2.cloned.1.call-done = bf16[8,512]{1,0:T(8,128)(2,1)} async-done(((bf16[8,2048]{1,0:T(8,128)(2,1)}), bf16[8,512]{1,0:T(8,128)(2,1)}) %reduce-scatter.2.cloned.1.call-update) | async-done | bytes 8208 | tf_op jit(solution)/shard_map/reduce_scatter | solution.py:162
  362.5 1.3 add_convert_fusion
  (89 shorter events, 6.0 us)
Async XLA Ops:
  6.5 2.9 copy-start
  6.5 80.0 %all-gather.7.cloned.1.call-start = ((), (), s32[]{:S(2)}) async-start(), calls=%async_computation.1 | async-start | bytes 1966080 | tf_op jit(solution)/shard_map/all_gather | solution.py:118
  7.3 81.1 %all-gather.9.cloned.1.call-start = ((), (), s32[]{:S(2)}) async-start(), calls=%async_computation.2 | async-start | bytes 2621440 | tf_op jit(solution)/shard_map/all_gather | solution.py:124
  8.0 124.1 %all-gather.11.cloned.1.call-start = ((), (), s32[]{:S(2)}) async-start(), calls=%async_computation.3 | async-start | bytes 2621440 | tf_op jit(solution)/shard_map/all_gather | solution.py:129
  8.7 170.7 %all-gather.13.cloned.1.call-start = ((), (), s32[]{:S(2)}) async-start(), calls=%async_computation.4 | async-start | bytes 2621440 | tf_op jit(solution)/shard_map/all_gather | solution.py:143
  9.3 1.7 copy-start.2
  9.3 19.7 %copy-start.4 = (bf16[8,2048]{1,0:T(8,128)(2,1)S(1)}, bf16[8,2048]{1,0:T(8,128)(2,1)}, u32[]{:S(2)}) copy-start(bf16[8,2048]{1,0:T(8,128)(2,1)} %param.17) | copy-start | bytes 98308
  9.3 285.8 %all-gather.15.cloned.1.call-start = ((), (), s32[]{:S(2)}) async-start(), calls=%async_computation.5 | async-start | bytes 7864320 | tf_op jit(solution)/shard_map/all_gather | solution.py:147
  11.0 330.3 %all-gather.17.cloned.1.call-start = ((), (), s32[]{:S(2)}) async-start(), calls=%async_computation.6 | async-start | bytes 2621440 | tf_op jit(solution)/shard_map/all_gather | solution.py:161
  11.1 17.9 %collective-permute-start = (bf16[512,512]{1,0:T(8,128)(2,1)S(1)}, bf16[512,512]{1,0:T(8,128)(2,1)S(1)}, u32[]{:S(2)}, u32[]{:S(2)}) collective-permute-start(bf16[512,512]{1,0:T(8,128)(2,1)S(1)} %copy-done.2), channel_id=1, source_target_pairs={{0,4},{4,8},{8,12},{12,0},{1,5},{5,9},{9,13},{13,1},{2,6},{6,10},{... | collective-permute-start | bytes 1572872 | tf_op jit(solution)/shard_map/ppermute | solution.py:25
  14.1 24.8 %collective-permute-start.2 = (bf16[512,512]{1,0:T(8,128)(2,1)S(1)}, bf16[512,512]{1,0:T(8,128)(2,1)S(1)}, u32[]{:S(2)}, u32[]{:S(2)}) collective-permute-start(bf16[512,512]{1,0:T(8,128)(2,1)S(1)} %copy-done.2), channel_id=1, source_target_pairs={{4,0},{8,4},{12,8},{0,12},{5,1},{9,5},{13,9},{1,13},{6,2},{10,6},{... | collective-permute-start | bytes 1572872 | tf_op jit(solution)/shard_map/ppermute | solution.py:27
  16.3 346.2 %reduce-scatter.2.cloned.1.call-start = ((), (), s32[]{:S(2)}) async-start(), calls=%async_computation.7 | async-start | bytes 40960 | tf_op jit(solution)/shard_map/reduce_scatter | solution.py:162
  29.0 29.4 %collective-permute-start.1 = (bf16[512,512]{1,0:T(8,128)(2,1)S(1)}, bf16[512,512]{1,0:T(8,128)(2,1)S(1)}, u32[]{:S(2)}, u32[]{:S(2)}) collective-permute-start(bf16[512,512]{1,0:T(8,128)(2,1)S(1)} %collective-permute-done), channel_id=1, source_target_pairs={{0,4},{4,8},{8,12},{12,0},{1,5},{5,9},{9,13},{13,1},{2,6},{6,10},{... | collective-permute-start | bytes 1572872 | tf_op jit(solution)/shard_map/ppermute | solution.py:25
  39.0 19.4 %copy-start.3 = (bf16[512,512]{1,0:T(8,128)(2,1)}, bf16[512,512]{1,0:T(8,128)(2,1)S(1)}, u32[]{:S(2)}) copy-start(bf16[512,512]{1,0:T(8,128)(2,1)S(1)} %collective-permute-done.2) | copy-start | bytes 1572868
  59.7 2.0 copy-start.5
  61.7 26.7 %copy-start.8 = (f32[2048]{0:T(1024)S(1)}, f32[2048]{0:T(1024)}, u32[]{:S(2)}) copy-start(f32[2048]{0:T(1024)} %param.19) | copy-start | bytes 24580
  88.4 3.3 copy-start.7
  88.4 43.7 %copy-start.1 = (bf16[384,2048]{1,0:T(8,128)(2,1)S(1)}, bf16[384,2048]{1,0:T(8,128)(2,1)}, u32[]{:S(2)}) copy-start(bf16[384,2048]{1,0:T(8,128)(2,1)} %all-gather.7.cloned.1.call-done) | copy-start | bytes 4718596
  168.2 127.0 %copy-start.6 = (f32[2048]{0:T(1024)S(1)}, f32[2048]{0:T(1024)}, u32[]{:S(2)}) copy-start(f32[2048]{0:T(1024)} %param.21) | copy-start | bytes 24580
Sparse Core Ops, SparseCore 0:
  8.9 22.3 all-gather.6
  32.9 52.4 all-gather.8
  86.9 45.1 all-gather.10
  133.5 45.9 all-gather.12
  180.9 114.2 all-gather.14
  296.6 44.6 all-gather.16
  344.3 18.1 reduce-scatter.1
